TPU v7x, 32 devices: a whole 2x2x4 slice. The times are simulated.
32 devices in a mesh: dp: 16 (over z, x, core), tensor: 2 (over y).
Axes of the slice: x: 2, y: 2, z: 4, core: 2. Of those that a mesh axis runs over, the one named last changes fastest.
Arguments:
- tokens: bfloat16 [8192, 640], P(('dp', 'tensor')), may hold values from -40 to 40
- cotangent: bfloat16 [8192, 640], P(('dp', 'tensor')), may hold values from -16 to 16
- positions: int32 [8192], P('dp'), may hold values from 0 to 1023, as said below
- w_query: bfloat16 [640, 1024], P('dp', 'tensor'), may hold values from -0.25 to 0.25
- w_key: bfloat16 [640, 256], P('dp'), may hold values from -0.25 to 0.25
- w_value: bfloat16 [640, 256], P('dp'), may hold values from -0.25 to 0.25
- w_out: bfloat16 [640, 1024], P('dp', 'tensor'), may hold values from -0.1875 to 0.1875
- w_gate: bfloat16 [640, 2048], P('dp', 'tensor'), may hold values from -0.25 to 0.25
- w_up: bfloat16 [640, 2048], P('dp', 'tensor'), may hold values from -0.25 to 0.25
- w_down: bfloat16 [640, 2048], P('dp', 'tensor'), may hold values from -0.125 to 0.125
- attn_in_gain: bfloat16 [640], replicated, may hold values from 0.25 to 1.75
- attn_out_gain: bfloat16 [640], replicated, may hold values from 0.25 to 1.75
- ffn_in_gain: bfloat16 [640], replicated, may hold values from 0.25 to 1.75
- ffn_out_gain: bfloat16 [640], replicated, may hold values from 0.25 to 1.75
- query_gain: bfloat16 [256], replicated, may hold values from 1 to 2
- key_gain: bfloat16 [256], replicated, may hold values from 1 to 2
Outputs:
- output: float32 [8192, 640], P(('dp', 'tensor'))
- input_grad: float32 [8192, 640], P(('dp', 'tensor'))
- grad_query: float32 [640, 1024], P('dp', 'tensor')
- grad_key: float32 [640, 256], P('dp')
- grad_value: float32 [640, 256], P('dp')
- grad_out: float32 [640, 1024], P('dp', 'tensor')
- grad_gate: float32 [640, 2048], P('dp', 'tensor')
- grad_up: float32 [640, 2048], P('dp', 'tensor')
- grad_down: float32 [640, 2048], P('dp', 'tensor')
- grad_attn_in_gain: float32 [640], replicated
- grad_attn_out_gain: float32 [640], replicated
- grad_ffn_in_gain: float32 [640], replicated
- grad_ffn_out_gain: float32 [640], replicated
- grad_query_gain: float32 [256], replicated
- grad_key_gain: float32 [256], replicated
Inputs may be any that keep to these rules, and one draw needn't show every extreme that they name: positions[t] is 0 where a document begins and positions[t - 1] + 1 elsewhere; a document begins at t = 0 and at every t with t % 1024 == 640; any other beginning lies at a t with t // 1024 odd and 640 < t % 1024 < 768.
All inputs are finite; a program needn't handle non-finite values.
Results may differ from a plain program's by a relative error of at most 0.018.
The roundings to bfloat16 on the way count: a program that leaves them out, or rounds other values in their place, can miss the bound.
Values may be sent and summed in bfloat16 or wider, within the bound.
No kernel may reach another device: no remote copies, remote signals or barrier semaphores. Data moves between devices by JAX's collectives and lax.ppermute only.
A program may use at most 128 MiB of HBM per device.

v0:
```python
import math
import jax
import jax.numpy as jnp
from jax import lax
from jax.sharding import PartitionSpec as P

HEAD_DIM = 256
WINDOW = 512
NORM_EPS = 1e-06
GELU_COEF = math.sqrt(2.0 / math.pi)


def shifted(value, axis, steps):
    count = lax.axis_size(axis)
    leading, last = (max(0, -steps), min(count, count - steps))
    return lax.ppermute(value, axis, [(source, source + steps) for source in range(leading, last)])


def norm_fwd(values, gain_vec):
    scale_inv = lax.rsqrt(jnp.mean(values * values, axis=-1, keepdims=True) + NORM_EPS)
    return (values * scale_inv * gain_vec, scale_inv)


def norm_bwd(values, scale_inv, gain_vec, upstream):
    scaled = upstream * gain_vec
    cube_inv = scale_inv * scale_inv * scale_inv
    inner_mean = jnp.mean(scaled * values, axis=-1, keepdims=True)
    return (scale_inv * scaled - values * cube_inv * inner_mean, upstream * values * scale_inv)


def rotary_tables(places):
    halfway = HEAD_DIM // 2
    frequency = jnp.exp(
        jnp.arange(halfway, dtype=jnp.float32) * (-2.0 * math.log(10000.0) / HEAD_DIM)
    )
    angles = places.astype(jnp.float32)[:, None] * frequency[None, :]
    return (jnp.cos(angles), jnp.sin(angles))


def rotate(inputs, cos_tab, sin_tab):
    halfway = inputs.shape[-1] // 2
    leading = inputs[..., :halfway]
    trailing = inputs[..., halfway:]
    return jnp.concatenate(
        [leading * cos_tab - trailing * sin_tab, trailing * cos_tab + leading * sin_tab], axis=-1
    )


def rotate_back(inputs, cos_tab, sin_tab):
    halfway = inputs.shape[-1] // 2
    leading = inputs[..., :halfway]
    trailing = inputs[..., halfway:]
    return jnp.concatenate(
        [leading * cos_tab + trailing * sin_tab, trailing * cos_tab - leading * sin_tab], axis=-1
    )


def gelu_parts(preact):
    inner_arg = GELU_COEF * (preact + 0.044715 * preact * preact * preact)
    tanh_val = jnp.tanh(inner_arg)
    gelu_val = 0.5 * preact * (1.0 + tanh_val)
    gelu_slope = 0.5 * (1.0 + tanh_val) + 0.5 * preact * (1.0 - tanh_val * tanh_val) * GELU_COEF * (
        1.0 + 3.0 * 0.044715 * preact * preact
    )
    return (gelu_val, gelu_slope)


def window_mask(places, window):
    query_idx = jnp.arange(window, dtype=jnp.int32)[:, None]
    key_idx = jnp.arange(2 * window, dtype=jnp.int32)[None, :]
    distance = query_idx + window - key_idx
    return (distance >= 0) & (distance < window) & (distance <= places[:, None])


def mul_plain(lhs_mat, rhs_mat):
    return jnp.dot(lhs_mat, rhs_mat, preferred_element_type=jnp.float32)


def mul_t(lhs_mat, rhs_mat):
    return lax.dot_general(
        lhs_mat, rhs_mat, (((1,), (1,)), ((), ())), preferred_element_type=jnp.float32
    )


def mul_tn(lhs_mat, rhs_mat):
    return lax.dot_general(
        lhs_mat, rhs_mat, (((0,), (0,)), ((), ())), preferred_element_type=jnp.float32
    )


def on_device(
    tokens,
    cotangent,
    positions,
    w_query,
    w_key,
    w_value,
    w_out,
    w_gate,
    w_up,
    w_down,
    attn_in_gain,
    attn_out_gain,
    ffn_in_gain,
    ffn_out_gain,
    query_gain,
    key_gain,
):
    own_rows = tokens.shape[0]
    group_rows = positions.shape[0]
    tensor_idx = lax.axis_index("tensor")
    score_scale = 1.0 / math.sqrt(HEAD_DIM)
    blocks = group_rows // WINDOW
    block_ids = jnp.arange(blocks, dtype=jnp.int32)
    gain_in = attn_in_gain.astype(jnp.float32)
    gain_pa = attn_out_gain.astype(jnp.float32)
    gain_pf = ffn_in_gain.astype(jnp.float32)
    gain_po = ffn_out_gain.astype(jnp.float32)
    gain_query = query_gain.astype(jnp.float32)
    gain_key = key_gain.astype(jnp.float32)

    def fetch_weights():
        return (
            lax.all_gather(w_query, "dp", axis=0, tiled=True),
            lax.all_gather(w_key, "dp", axis=0, tiled=True),
            lax.all_gather(w_value, "dp", axis=0, tiled=True),
            lax.all_gather(w_out, "dp", axis=0, tiled=True),
            lax.all_gather(w_gate, "dp", axis=0, tiled=True),
            lax.all_gather(w_up, "dp", axis=0, tiled=True),
            lax.all_gather(w_down, "dp", axis=0, tiled=True),
        )

    def reduce_grads(first_grad, second_grad, third_grad):
        return (
            lax.psum_scatter(first_grad, "dp", scatter_dimension=0, tiled=True),
            lax.psum_scatter(second_grad, "dp", scatter_dimension=0, tiled=True),
            lax.psum_scatter(third_grad, "dp", scatter_dimension=0, tiled=True),
        )

    def own_slice(whole, offset, row_count):
        return lax.dynamic_slice_in_dim(whole, offset, row_count, 0)

    front_weights = fetch_weights()
    full_query, full_key, full_value, full_out, full_gate, full_up, full_down = front_weights
    heads_local = full_query.shape[1] // HEAD_DIM
    inputs_f = tokens.astype(jnp.float32)
    normed_own, inv_in = norm_fwd(inputs_f, gain_in)
    normed_in = lax.all_gather(normed_own.astype(jnp.bfloat16), "tensor", axis=0, tiled=True)
    raw_query = mul_plain(normed_in, full_query).reshape(group_rows, heads_local, HEAD_DIM)
    raw_key = mul_plain(normed_in, full_key)
    raw_value = mul_plain(normed_in, full_value)
    unit_query, inv_query = norm_fwd(raw_query, gain_query)
    unit_key, inv_key = norm_fwd(raw_key, gain_key)
    cos_tab, sin_tab = rotary_tables(positions)
    rot_query = rotate(unit_query, cos_tab[:, None, :], sin_tab[:, None, :]).astype(jnp.bfloat16)
    rot_key = rotate(unit_key, cos_tab, sin_tab).astype(jnp.bfloat16)
    value_b = raw_value.astype(jnp.bfloat16)
    halo_key, halo_value = shifted((rot_key, value_b), "dp", 1)
    keys_ext = jnp.concatenate([halo_key, rot_key], axis=0)
    values_ext = jnp.concatenate([halo_value, value_b], axis=0)

    def block_scores(block_idx):
        offset = block_idx * WINDOW
        allowed = window_mask(positions, WINDOW)[None]
        scores = (
            jnp.einsum("qhd,kd->hqk", rot_query, keys_ext, preferred_element_type=jnp.float32)
            * score_scale
        )
        return (rot_query, keys_ext, values_ext, jnp.where(allowed, scores, -1e30), offset)

    def attend(unused, block_idx):
        queries, keys_blk, values_blk, masked, offset = block_scores(block_idx)
        row_max = jnp.max(masked, axis=-1, keepdims=True)
        weights_exp = jnp.exp(masked - row_max)
        row_sum = jnp.sum(weights_exp, axis=-1, keepdims=True)
        probs_b = (weights_exp / row_sum).astype(jnp.bfloat16)
        mixed_blk = jnp.einsum(
            "hqk,kd->qhd", probs_b, values_blk, preferred_element_type=jnp.float32
        ).astype(jnp.bfloat16)
        return (unused, (mixed_blk, (row_max + jnp.log(row_sum))[..., 0]))

    mixed_parts, lse_parts = lax.scan(attend, jnp.zeros((), jnp.float32), block_ids)[1]
    mixed_heads = mixed_parts.reshape(group_rows, heads_local, HEAD_DIM)
    attn_mixed = mixed_parts.reshape(group_rows, heads_local * HEAD_DIM)
    attn_proj = lax.psum_scatter(
        mul_t(own_slice(attn_mixed, jnp.int32(0), own_rows * lax.axis_size("tensor")), full_out),
        "tensor",
        scatter_dimension=0,
        tiled=True,
    )
    attn_norm, inv_pa = norm_fwd(attn_proj, gain_pa)
    residual = inputs_f + attn_norm
    ffn_in_f, inv_pf = norm_fwd(residual, gain_pf)
    normed_ffn = lax.all_gather(ffn_in_f.astype(jnp.bfloat16), "tensor", axis=0, tiled=True)
    gate_proj = mul_plain(normed_ffn, full_gate)
    up_proj = mul_plain(normed_ffn, full_up)
    gelu_val, gelu_slope = gelu_parts(gate_proj)
    hidden = (gelu_val * up_proj).astype(jnp.bfloat16)
    ffn_raw = lax.psum_scatter(
        mul_t(own_slice(hidden, jnp.int32(0), own_rows * lax.axis_size("tensor")), full_down),
        "tensor",
        scatter_dimension=0,
        tiled=True,
    )
    ffn_norm, inv_po = norm_fwd(ffn_raw, gain_po)
    output = residual + ffn_norm
    back_weights = fetch_weights()
    back_query, back_key, back_value, back_out, back_gate, back_up, back_down = back_weights
    upstream = cotangent.astype(jnp.float32)
    ffn_cot_f, po_terms = norm_bwd(ffn_raw, inv_po, gain_po, upstream)
    ffn_cot = lax.all_gather(ffn_cot_f.astype(jnp.bfloat16), "tensor", axis=0, tiled=True)
    grad_down = mul_tn(ffn_cot, hidden)
    hidden_cot = mul_plain(ffn_cot, back_down)
    gate_cot = (hidden_cot * up_proj * gelu_slope).astype(jnp.bfloat16)
    up_cot = (hidden_cot * gelu_val).astype(jnp.bfloat16)
    grad_gate = mul_tn(normed_ffn, gate_cot)
    grad_up = mul_tn(normed_ffn, up_cot)
    ffn_grads = (grad_gate, grad_up, grad_down)
    offset = jnp.int32(0)
    ffn_in_cot = lax.psum_scatter(
        mul_t(own_slice(gate_cot, offset, own_rows * lax.axis_size("tensor")), back_gate)
        + mul_t(own_slice(up_cot, offset, own_rows * lax.axis_size("tensor")), back_up),
        "tensor",
        scatter_dimension=0,
        tiled=True,
    )
    resid_back, pf_terms = norm_bwd(residual, inv_pf, gain_pf, ffn_in_cot)
    resid_cot = upstream + resid_back
    attn_cot_f, pa_terms = norm_bwd(attn_proj, inv_pa, gain_pa, resid_cot)
    attn_cot = lax.all_gather(attn_cot_f.astype(jnp.bfloat16), "tensor", axis=0, tiled=True)
    grad_out = mul_tn(attn_cot, attn_mixed)
    mixed_cot = (
        mul_plain(attn_cot, back_out)
        .astype(jnp.bfloat16)
        .reshape(group_rows, heads_local, HEAD_DIM)
    )

    def attend_back(carried, block_idx):
        key_ext_cot, value_ext_cot = carried
        queries, keys_blk, values_blk, masked, offset = block_scores(block_idx)
        lse_blk = lse_parts[block_idx]
        probs_f = jnp.exp(masked - lse_blk[..., None])
        delta_row = jnp.sum(
            mixed_cot.astype(jnp.float32) * mixed_heads.astype(jnp.float32), axis=-1
        )
        prob_cot = jnp.einsum(
            "qhd,kd->hqk", mixed_cot, values_blk, preferred_element_type=jnp.float32
        )
        score_cot = (probs_f * (prob_cot - jnp.transpose(delta_row)[:, :, None])).astype(
            jnp.bfloat16
        )
        query_cot = (
            jnp.einsum("hqk,kd->qhd", score_cot, keys_blk, preferred_element_type=jnp.float32)
            * score_scale
        )
        key_pair = (
            jnp.einsum("hqk,qhd->kd", score_cot, queries, preferred_element_type=jnp.float32)
            * score_scale
        )
        value_pair = jnp.einsum(
            "hqk,qhd->kd",
            probs_f.astype(jnp.bfloat16),
            mixed_cot,
            preferred_element_type=jnp.float32,
        )
        key_ext_cot = key_ext_cot + key_pair
        value_ext_cot = value_ext_cot + value_pair
        return ((key_ext_cot, value_ext_cot), query_cot)

    zero_ext = jnp.zeros((group_rows + WINDOW, HEAD_DIM), jnp.float32)
    ext_cots, query_parts = lax.scan(attend_back, (zero_ext, zero_ext), block_ids)
    key_ext_cot, value_ext_cot = ext_cots
    query_cot = query_parts.reshape(group_rows, heads_local, HEAD_DIM)
    back_key_cot, back_value_cot = shifted((key_ext_cot[:WINDOW], value_ext_cot[:WINDOW]), "dp", -1)
    own_key_cot = key_ext_cot[WINDOW:].at[group_rows - WINDOW :].add(back_key_cot)
    own_value_cot = value_ext_cot[WINDOW:].at[group_rows - WINDOW :].add(back_value_cot)
    key_cot, value_cot = lax.psum((own_key_cot, own_value_cot), "tensor")
    query_unit_cot = rotate_back(query_cot, cos_tab[:, None, :], sin_tab[:, None, :])
    query_raw_cot, qgain_terms = norm_bwd(raw_query, inv_query, gain_query, query_unit_cot)
    key_raw_cot, kgain_terms = norm_bwd(
        raw_key, inv_key, gain_key, rotate_back(key_cot, cos_tab, sin_tab)
    )
    query_proj_cot = query_raw_cot.reshape(group_rows, heads_local * HEAD_DIM).astype(jnp.bfloat16)
    keyval_cot = jnp.concatenate([key_raw_cot, value_cot], axis=1).astype(jnp.bfloat16)
    grad_query = mul_tn(normed_in, query_proj_cot)
    grad_keyval = mul_tn(normed_in, keyval_cot)
    attn_grads = reduce_grads(grad_query, grad_out, grad_keyval)
    ffn_done = reduce_grads(ffn_grads[0], ffn_grads[1], ffn_grads[2])
    in_query_cot = lax.psum_scatter(
        mul_t(
            own_slice(query_proj_cot, jnp.int32(0), own_rows * lax.axis_size("tensor")), back_query
        ),
        "tensor",
        scatter_dimension=0,
        tiled=True,
    )
    own_keyval = own_slice(keyval_cot, tensor_idx * own_rows, own_rows)
    in_cot = (
        in_query_cot
        + mul_t(own_keyval[:, :HEAD_DIM], back_key)
        + mul_t(own_keyval[:, HEAD_DIM:], back_value)
    )
    in_back, in_terms = norm_bwd(inputs_f, inv_in, gain_in, in_cot)
    input_grad = resid_cot + in_back
    own_kgain = own_slice(kgain_terms, tensor_idx * own_rows, own_rows)
    gain_totals = lax.psum(
        (
            jnp.sum(in_terms, axis=0),
            jnp.sum(pa_terms, axis=0),
            jnp.sum(pf_terms, axis=0),
            jnp.sum(po_terms, axis=0),
            jnp.sum(qgain_terms, axis=(0, 1)),
            jnp.sum(own_kgain, axis=0),
        ),
        ("dp", "tensor"),
    )
    red_query, red_out, red_keyval = attn_grads
    red_gate, red_up, red_down = ffn_done
    return (
        output,
        input_grad,
        red_query,
        red_keyval[:, :HEAD_DIM],
        red_keyval[:, HEAD_DIM:],
        red_out,
        red_gate,
        red_up,
        red_down,
        gain_totals[0],
        gain_totals[1],
        gain_totals[2],
        gain_totals[3],
        gain_totals[4],
        gain_totals[5],
    )


def solution(mesh):
    placed = (
        P(("dp", "tensor"), None),
        P(("dp", "tensor"), None),
        P("dp"),
        P("dp", "tensor"),
        P("dp", None),
        P("dp", None),
        P("dp", "tensor"),
        P("dp", "tensor"),
        P("dp", "tensor"),
        P("dp", "tensor"),
        P(),
        P(),
        P(),
        P(),
        P(),
        P(),
    )
    return jax.shard_map(
        on_device,
        mesh=mesh,
        in_specs=placed,
        out_specs=(
            P(("dp", "tensor"), None),
            P(("dp", "tensor"), None),
            P("dp", "tensor"),
            P("dp", None),
            P("dp", None),
            P("dp", "tensor"),
            P("dp", "tensor"),
            P("dp", "tensor"),
            P("dp", "tensor"),
            P(),
            P(),
            P(),
            P(),
            P(),
            P(),
        ),
        check_vma=False,
    )
```

profile of v0, /device:TPU:0, one launch (start us, length us, event | category | flops | bytes accessed | tf_op | source)
XLA Modules:
  0.0 803.0 jit_solution(5210754273820722378)
XLA Ops:
  10.5 24.2 %all_gather.41 = bf16[640,256]{1,0:T(8,128)(2,1)S(1)} all-gather(bf16[40,256]{1,0:T(8,128)(2,1)} %param.29), channel_id=1, replica_groups=mesh['dp'=16,'tensor'=2] {'dp'}, dimensions={0}, use_global_device_ids=true | all-gather | bytes 348160 | tf_op jit(solution)/shard_map/all_gather | solution.py:126
  35.9 10.6 %all_gather.40 = bf16[512,640]{1,0:T(8,128)(2,1)S(1)} all-gather(bf16[256,640]{1,0:T(8,128)(2,1)S(1)} %fusion.42), channel_id=1, replica_groups=mesh['dp'=16,'tensor'=2] {'tensor'}, dimensions={0}, use_global_device_ids=true | all-gather | bytes 983040 | tf_op jit(solution)/shard_map/all_gather | solution.py:148
  49.8 18.0 %all_gather.42 = bf16[640,256]{1,0:T(8,128)(2,1)S(1)} all-gather(bf16[40,256]{1,0:T(8,128)(2,1)S(1)} %copy-done.59), channel_id=1, replica_groups=mesh['dp'=16,'tensor'=2] {'dp'}, dimensions={0}, use_global_device_ids=true | all-gather | bytes 348160 | tf_op jit(solution)/shard_map/all_gather | solution.py:125
  71.0 3.0 collective-permute-start.1
  76.1 20.4 %all_gather.43 = bf16[640,512]{1,0:T(8,128)(2,1)S(1)} all-gather(bf16[40,512]{1,0:T(8,128)(2,1)S(1)} %copy-done.57), channel_id=1, replica_groups=mesh['dp'=16,'tensor'=2] {'dp'}, dimensions={0}, use_global_device_ids=true | all-gather | bytes 696320 | tf_op jit(solution)/shard_map/all_gather | solution.py:124
  96.5 21.2 %all_gather.44 = bf16[640,512]{1,0:T(8,128)(2,1)} all-gather(bf16[40,512]{1,0:T(8,128)(2,1)S(1)} %copy-done.58), channel_id=1, replica_groups=mesh['dp'=16,'tensor'=2] {'dp'}, dimensions={0}, use_global_device_ids=true | all-gather | bytes 696320 | tf_op jit(solution)/shard_map/all_gather | solution.py:127
  124.9 3.1 fusion.29
  132.4 19.5 %reduce-scatter.11.cloned.1.call-done = f32[256,640]{1,0:T(8,128)} async-done(((f32[512,640]{1,0:T(8,128)}), f32[256,640]{1,0:T(8,128)}) %reduce-scatter.11.cloned.1.call-update) | async-done | bytes 655376 | tf_op jit(solution)/shard_map/reduce_scatter | solution.py:185
  154.6 10.1 %all_gather.45 = bf16[512,640]{1,0:T(8,128)(2,1)S(1)} all-gather(bf16[256,640]{1,0:T(8,128)(2,1)S(1)} %multiply_convert_fusion.2), channel_id=1, replica_groups=mesh['dp'=16,'tensor'=2] {'tensor'}, dimensions={0}, use_global_device_ids=true | all-gather | bytes 983040 | tf_op jit(solution)/shard_map/all_gather | solution.py:194
  164.7 5.0 all-gather.4.cloned.1.call-done
  169.7 3.7 fusion.85
  173.4 36.2 %all-gather.6.cloned.1.call-done = bf16[640,1024]{1,0:T(8,128)(2,1)} async-done(((bf16[40,1024]{1,0:T(8,128)(2,1)}), bf16[640,1024]{1,0:T(8,128)(2,1)}) %all-gather.6.cloned.1.call-update) | async-done | bytes 1310736 | tf_op jit(solution)/shard_map/all_gather | solution.py:129
  209.6 4.9 multiply_convert_fusion.1
  214.5 34.9 %all-gather.8.cloned.1.call-done = bf16[640,1024]{1,0:T(8,128)(2,1)} async-done(((bf16[40,1024]{1,0:T(8,128)(2,1)}), bf16[640,1024]{1,0:T(8,128)(2,1)}) %all-gather.8.cloned.1.call-update) | async-done | bytes 1310736 | tf_op jit(solution)/shard_map/all_gather | solution.py:130
  249.4 3.7 fusion.86
  253.2 22.2 %reduce-scatter.13.cloned.1.call-done = f32[256,640]{1,0:T(8,128)} async-done(((f32[512,640]{1,0:T(8,128)}), f32[256,640]{1,0:T(8,128)}) %reduce-scatter.13.cloned.1.call-update) | async-done | bytes 655376 | tf_op jit(solution)/shard_map/reduce_scatter | solution.py:199
  280.4 9.9 %all_gather.49 = bf16[512,640]{1,0:T(8,128)(2,1)S(1)} all-gather(bf16[256,640]{1,0:T(8,128)(2,1)S(1)} %get-tuple-element.136), channel_id=1, replica_groups=mesh['dp'=16,'tensor'=2] {'tensor'}, dimensions={0}, use_global_device_ids=true | all-gather | bytes 983040 | tf_op jit(solution)/shard_map/all_gather | solution.py:211
  290.4 3.9 multiply_convert_fusion
  298.6 23.3 %reduce-scatter.15.cloned.1.call-done = f32[256,640]{1,0:T(8,128)} async-done(((f32[512,640]{1,0:T(8,128)}), f32[256,640]{1,0:T(8,128)}) %reduce-scatter.15.cloned.1.call-update) | async-done | bytes 655376 | tf_op jit(solution)/shard_map/reduce_scatter | solution.py:220
  325.2 10.1 %all_gather.50 = bf16[512,640]{1,0:T(8,128)(2,1)S(1)} all-gather(bf16[256,640]{1,0:T(8,128)(2,1)S(1)} %subtract_convert_fusion), channel_id=1, replica_groups=mesh['dp'=16,'tensor'=2] {'tensor'}, dimensions={0}, use_global_device_ids=true | all-gather | bytes 983040 | tf_op jit(solution)/shard_map/all_gather | solution.py:230
  336.0 2.8 fusion.1
  354.9 3.6 fusion.25
  359.8 7.9 collective-permute-done.3
  367.8 21.2 %all-reduce.5 = bf16[512,256]{0,1:T(8,128)(2,1)S(1)} all-reduce(f32[512,256]{0,1:T(8,128)S(1)} %slice_add_fusion), channel_id=1, replica_groups=mesh['dp'=16,'tensor'=2] {'tensor'}, use_global_device_ids=true, to_apply=%region_19.20 | all-reduce | flops 131072 | bytes 786432 | tf_op jit(solution)/shard_map/psum | solution.py:277
  394.7 3.6 fusion.93
  413.8 44.8 %all-reduce = (f32[640]{0:T(1024)}, f32[640]{0:T(1024)}, f32[640]{0:T(1024)}, f32[640]{0:T(1024)}, f32[256]{0:T(256)}, /*index=5*/f32[256]{0:T(256)}) all-reduce(f32[640]{0:T(1024)S(1)} %get-tuple-element.115, f32[640]{0:T(1024)S(1)} %get-tuple-element.111, ...), channel_id=1, replica_groups=mesh['dp'=16,'tensor'=2] {'dp','tensor'}, use_global_device_ids=true, to_apply=%region_28.29 | all-reduce | flops 3072 | bytes 24576 | tf_op jit(solution)/shard_map/psum | solution.py:306
  459.7 9.7 %reduce-scatter.21.cloned.1.call-done = f32[40,512]{1,0:T(8,128)} async-done(((f32[640,512]{1,0:T(8,128)}), f32[40,512]{1,0:T(8,128)}) %reduce-scatter.21.cloned.1.call-update) | async-done | bytes 81936 | tf_op jit(solution)/shard_map/reduce_scatter | solution.py:137
  470.8 66.1 %reduce-scatter.29.cloned.1.call-done = f32[40,1024]{1,0:T(8,128)} async-done(((f32[640,1024]{1,0:T(8,128)}), f32[40,1024]{1,0:T(8,128)}) %reduce-scatter.29.cloned.1.call-update) | async-done | bytes 163856 | tf_op jit(solution)/shard_map/reduce_scatter | solution.py:137
  536.9 67.6 %reduce-scatter.27.cloned.1.call-done = f32[40,1024]{1,0:T(8,128)} async-done(((f32[640,1024]{1,0:T(8,128)}), f32[40,1024]{1,0:T(8,128)}) %reduce-scatter.27.cloned.1.call-update) | async-done | bytes 163856 | tf_op jit(solution)/shard_map/reduce_scatter | solution.py:136
  604.5 67.6 %reduce-scatter.25.cloned.1.call-done = f32[40,1024]{1,0:T(8,128)} async-done(((f32[640,1024]{1,0:T(8,128)}), f32[40,1024]{1,0:T(8,128)}) %reduce-scatter.25.cloned.1.call-update) | async-done | bytes 163856 | tf_op jit(solution)/shard_map/reduce_scatter | solution.py:135
  672.1 61.7 %reduce-scatter.23.cloned.1.call-done = f32[40,512]{1,0:T(8,128)} async-done(((f32[640,512]{1,0:T(8,128)}), f32[40,512]{1,0:T(8,128)}) %reduce-scatter.23.cloned.1.call-update) | async-done | bytes 81936 | tf_op jit(solution)/shard_map/reduce_scatter | solution.py:136
  733.8 61.9 %reduce-scatter.19.cloned.1.call-done = f32[40,512]{1,0:T(8,128)} async-done(((f32[640,512]{1,0:T(8,128)}), f32[40,512]{1,0:T(8,128)}) %reduce-scatter.19.cloned.1.call-update) | async-done | bytes 81936 | tf_op jit(solution)/shard_map/reduce_scatter | solution.py:135
  (283 shorter events, 79.8 us)
Async XLA Ops:
  8.0 41.7 %copy-start.78 = (bf16[256]{0:T(256)(128)(2,1)S(1)}, bf16[256]{0:T(256)(128)(2,1)}, u32[]{:S(2)}) copy-start(bf16[256]{0:T(256)(128)(2,1)} %param.39) | copy-start | bytes 1540
  8.0 41.7 %copy-start.67 = (s32[512]{0:T(512)S(1)}, s32[512]{0:T(512)}, u32[]{:S(2)}) copy-start(s32[512]{0:T(512)} %param.26) | copy-start | bytes 6148
  8.0 41.8 %copy-start.59 = (bf16[40,256]{1,0:T(8,128)(2,1)S(1)}, bf16[40,256]{1,0:T(8,128)(2,1)}, u32[]{:S(2)}) copy-start(bf16[40,256]{1,0:T(8,128)(2,1)} %param.28) | copy-start | bytes 61444
  8.0 143.8 %reduce-scatter.11.cloned.1.call-start = ((), (), s32[]{:S(2)}) async-start(), calls=%async_computation.10 | async-start | bytes 1966080 | tf_op jit(solution)/shard_map/reduce_scatter | solution.py:185
  9.8 40.0 %copy-start.60 = (f32[256]{0:T(256)}, f32[256]{0:T(256)S(1)}, u32[]{:S(2)}) copy-start(f32[256]{0:T(256)S(1)} %get-tuple-element.151) | copy-start | bytes 3076
  47.6 77.3 %collective-permute-start = (bf16[512,256]{1,0:T(8,128)(2,1)}, bf16[512,256]{1,0:T(8,128)(2,1)}, u32[]{:S(2)}, u32[]{:S(2)}) collective-permute-start(bf16[512,256]{1,0:T(8,128)(2,1)} %convolution_convert_fusion.1), channel_id=1, source_target_pairs={{0,2},{2,4},{4,6},{6,8},{8,10},{10,12},{12,14},{14,16},{16,18},{18... | collective-permute-start | bytes 786440 | tf_op jit(solution)/shard_map/ppermute | solution.py:16
  68.9 27.6 %copy-start.58 = (bf16[40,512]{1,0:T(8,128)(2,1)S(1)}, bf16[40,512]{1,0:T(8,128)(2,1)}, u32[]{:S(2)}) copy-start(bf16[40,512]{1,0:T(8,128)(2,1)} %param.30) | copy-start | bytes 122884
  71.0 50.6 %collective-permute-start.1 = (bf16[512,256]{0,1:T(8,128)(2,1)}, bf16[512,256]{0,1:T(8,128)(2,1)}, u32[]{:S(2)}, u32[]{:S(2)}) collective-permute-start(bf16[512,256]{0,1:T(8,128)(2,1)} %pad_maximum_fusion.7), channel_id=1, source_target_pairs={{0,2},{2,4},{4,6},{6,8},{8,10},{10,12},{12,14},{14,16},{16,18},{18... | collective-permute-start | bytes 786440 | tf_op jit(solution)/shard_map/ppermute | solution.py:16
  75.2 45.4 %copy-start.33 = (f32[512,128]{1,0:T(8,128)}, f32[512,128]{1,0:T(8,128)S(1)}, u32[]{:S(2)}) copy-start(f32[512,128]{1,0:T(8,128)S(1)} %copy.49) | copy-start | bytes 786436
  96.5 22.5 %copy-start.8 = (bf16[640,512]{1,0:T(8,128)(2,1)}, bf16[640,512]{1,0:T(8,128)(2,1)S(1)}, u32[]{:S(2)}) copy-start(bf16[640,512]{1,0:T(8,128)(2,1)S(1)} %all_gather.43) | copy-start | bytes 1966084
  128.8 24.3 %copy-start.5 = (bf16[256,640]{1,0:T(8,128)(2,1)S(1)}, bf16[256,640]{1,0:T(8,128)(2,1)}, u32[]{:S(2)}) copy-start(bf16[256,640]{1,0:T(8,128)(2,1)} %param.24) | copy-start | bytes 983044
  130.5 39.2 %all-gather.4.cloned.1.call-start = ((), (), s32[]{:S(2)}) async-start(), calls=%async_computation.11 | async-start | bytes 1392640 | tf_op jit(solution)/shard_map/all_gather | solution.py:128
  131.1 78.5 %all-gather.6.cloned.1.call-start = ((), (), s32[]{:S(2)}) async-start(), calls=%async_computation.12 | async-start | bytes 1392640 | tf_op jit(solution)/shard_map/all_gather | solution.py:129
  131.7 117.7 %all-gather.8.cloned.1.call-start = ((), (), s32[]{:S(2)}) async-start(), calls=%async_computation.13 | async-start | bytes 1392640 | tf_op jit(solution)/shard_map/all_gather | solution.py:130
  132.3 143.2 %reduce-scatter.13.cloned.1.call-start = ((), (), s32[]{:S(2)}) async-start(), calls=%async_computation.14 | async-start | bytes 1966080 | tf_op jit(solution)/shard_map/reduce_scatter | solution.py:199
  253.2 68.8 %reduce-scatter.15.cloned.1.call-start = ((), (), s32[]{:S(2)}) async-start(), calls=%async_computation.15 | async-start | bytes 1966080 | tf_op jit(solution)/shard_map/reduce_scatter | solution.py:220
  298.5 24.7 %copy-start = (f32[256,640]{1,0:T(8,128)S(1)}, f32[256,640]{1,0:T(8,128)}, u32[]{:S(2)}) copy-start(f32[256,640]{1,0:T(8,128)} %reduce-scatter.11.cloned.1.call-done) | copy-start | bytes 1966084
  298.5 90.6 %all-reduce.4.cloned.1.call-start = ((), (), s32[]{:S(2)}) async-start(), calls=%async_computation.17 | async-start | bytes 1048576 | tf_op jit(solution)/shard_map/psum | solution.py:277
  339.7 4.6 collective-permute-start.2
  345.2 65.4 %reduce-scatter.17.cloned.1.call-start = ((), (), s32[]{:S(2)}) async-start(), calls=%async_computation.16 | async-start | bytes 1966080 | tf_op jit(solution)/shard_map/reduce_scatter | solution.py:289
  354.8 114.6 %reduce-scatter.21.cloned.1.call-start = ((), (), s32[]{:S(2)}) async-start(), calls=%async_computation.19 | async-start | bytes 1392640 | tf_op jit(solution)/shard_map/reduce_scatter | solution.py:137
  358.5 30.6 %copy-start.72 = (f32[128]{0:T(128)S(1)}, f32[128]{0:T(128)}, u32[]{:S(2)}) copy-start(f32[128]{0:T(128)} %copy-done.71) | copy-start | bytes 1540
  358.5 32.9 %copy-start.65 = (f32[256]{0:T(256)S(1)}, f32[256]{0:T(256)}, u32[]{:S(2)}) copy-start(f32[256]{0:T(256)} %copy-done.64) | copy-start | bytes 3076
  358.5 33.6 %copy-start.66 = (f32[512]{0:T(512)S(1)}, f32[512]{0:T(512)}, u32[]{:S(2)}) copy-start(f32[512]{0:T(512)} %get-tuple-element.148) | copy-start | bytes 6148
  358.5 9.2 %collective-permute-start.3 = (f32[512,256]{0,1:T(8,128)S(1)}, f32[512,256]{0,1:T(8,128)S(1)}, u32[]{:S(2)}, u32[]{:S(2)}) collective-permute-start(f32[512,256]{0,1:T(8,128)S(1)} %slice.103), channel_id=1, source_target_pairs={{2,0},{4,2},{6,4},{8,6},{10,8},{12,10},{14,12},{16,14},{18,16},{20... | collective-permute-start | bytes 1572872 | tf_op jit(solution)/shard_map/ppermute | solution.py:16
  394.6 142.3 %reduce-scatter.29.cloned.1.call-start = ((), (), s32[]{:S(2)}) async-start(), calls=%async_computation.23 | async-start | bytes 2785280 | tf_op jit(solution)/shard_map/reduce_scatter | solution.py:137
  398.3 206.3 %reduce-scatter.27.cloned.1.call-start = ((), (), s32[]{:S(2)}) async-start(), calls=%async_computation.22 | async-start | bytes 2785280 | tf_op jit(solution)/shard_map/reduce_scatter | solution.py:136
  401.9 270.2 %reduce-scatter.25.cloned.1.call-start = ((), (), s32[]{:S(2)}) async-start(), calls=%async_computation.21 | async-start | bytes 2785280 | tf_op jit(solution)/shard_map/reduce_scatter | solution.py:135
  405.5 328.3 %reduce-scatter.23.cloned.1.call-start = ((), (), s32[]{:S(2)}) async-start(), calls=%async_computation.20 | async-start | bytes 1392640 | tf_op jit(solution)/shard_map/reduce_scatter | solution.py:136
  408.4 387.3 %reduce-scatter.19.cloned.1.call-start = ((), (), s32[]{:S(2)}) async-start(), calls=%async_computation.18 | async-start | bytes 1392640 | tf_op jit(solution)/shard_map/reduce_scatter | solution.py:135
  410.5 48.1 %copy-start.7 = (f32[256,640]{1,0:T(8,128)S(1)}, f32[256,640]{1,0:T(8,128)}, u32[]{:S(2)}) copy-start(f32[256,640]{1,0:T(8,128)} %copy-done.6) | copy-start | bytes 1966084
  410.5 48.1 %copy-start.70 = (f32[256]{0:T(256)S(1)}, f32[256]{0:T(256)}, u32[]{:S(2)}) copy-start(f32[256]{0:T(256)} %get-tuple-element.150) | copy-start | bytes 3076
  (69 other events, 300.6 us)
Sparse Core Ops, SparseCore 0:
  130.7 21.1 reduce-scatter.10
  253.3 22.1 reduce-scatter.12
  298.6 23.2 reduce-scatter.14
  345.3 36.6 all-reduce.3
  384.1 22.8 reduce-scatter.16
  410.4 58.8 reduce-scatter.20
  473.7 63.1 reduce-scatter.28
  541.3 63.2 reduce-scatter.26
  608.9 63.2 reduce-scatter.24
  676.2 57.5 reduce-scatter.22
  738.0 57.6 reduce-scatter.18
Sparse Core Ops, SparseCore 1:
  133.3 36.4 all-gather.3
  171.9 37.7 all-gather.5
  211.8 37.6 all-gather.7
where the time goes:
time: 804 us; the launch traced here: 803 us
  waiting for transfers between devices  485 us (60%)
  blocking collectives  191 us (24%)
  matrix products  56 us (7%)
  other arithmetic  31.9 us (4%)
  between operations  16.8 us (2%)
  local copies, waits for them, and re-layouts  13.7 us (2%)
  starting transfers between devices  8.57 us (1%)
    reduce_scatter x2, waiting for transfers between devices, reduce_grads(): lax.psum_scatter(first_grad, 'dp', scatter_dimension=0, tiled=True)  129 us
    reduce_scatter x2, waiting for transfers between devices, reduce_grads(): lax.psum_scatter(second_grad, 'dp', scatter_dimension=0, tiled=True)  129 us
    reduce_scatter x2, waiting for transfers between devices, reduce_grads(): lax.psum_scatter(third_grad, 'dp', scatter_dimension=0, tiled=True)  75.8 us
    psum x1, blocking collectives, on_device(): lax.psum((jnp.sum(in_terms, axis=0), jnp.sum(pa_terms, axis=0), jnp.sum(p...  44.8 us
    all_gather x1, waiting for transfers between devices, fetch_weights(): lax.all_gather(w_up, 'dp', axis=0, tiled=True)  36.2 us
    all_gather x1, waiting for transfers between devices, fetch_weights(): lax.all_gather(w_down, 'dp', axis=0, tiled=True)  34.9 us
    all_gather x1, blocking collectives, fetch_weights(): lax.all_gather(w_value, 'dp', axis=0, tiled=True)  24.2 us
    reduce_scatter x1, waiting for transfers between devices, on_device(): lax.psum_scatter(mul_t(own_slice(gate_cot, offset, own_rows * lax.axis_si...  23.3 us
  transfers between devices with their start and end apart: 18, of which 13 were waited for; matrix products, arithmetic and copies ran while one was open for 7% of the time, Pallas kernels for 0%

commit v1 on v0

--- a/solution.py
+++ b/solution.py
@@ -8,6 +8,27 @@
 WINDOW = 512
 NORM_EPS = 1e-06
 GELU_COEF = math.sqrt(2.0 / math.pi)
+
+
+def joined_along(pieces, dim):
+    pieces = jnp.moveaxis(pieces, 0, dim)
+    lengths = pieces.shape
+    return pieces.reshape(*lengths[:dim], lengths[dim] * lengths[dim + 1], *lengths[dim + 2 :])
+
+
+def grow_blocks(x, axis):
+    count, index = (lax.axis_size(axis), lax.axis_index(axis))
+    parts, bit = (x[None], 1)
+    while bit < count:
+        theirs = lax.ppermute(parts, axis, [(i, i ^ bit) for i in range(count)])
+        low = index & bit == 0
+        parts = jnp.concatenate([jnp.where(low, parts, theirs), jnp.where(low, theirs, parts)])
+        bit *= 2
+    return parts
+
+
+def collect(x, axis, dim):
+    return joined_along(grow_blocks(x, axis), dim)
 
 
 def shifted(value, axis, steps):
@@ -121,7 +142,7 @@
 
     def fetch_weights():
         return (
-            lax.all_gather(w_query, "dp", axis=0, tiled=True),
+            collect(w_query, "dp", 0),
             lax.all_gather(w_key, "dp", axis=0, tiled=True),
             lax.all_gather(w_value, "dp", axis=0, tiled=True),
             lax.all_gather(w_out, "dp", axis=0, tiled=True),

time: 804 us -> 801 us (level)
  blocking collectives: 191 us -> 175 us
  waiting for transfers between devices: 485 us -> 495 us
    all_gather x1 -> x0, blocking collectives: 20.4 us -> none  [fetch_weights(): lax.all_gather(w_query, 'dp', axis=0, tiled=True)]
  transfers between devices with their start and end apart: 18 -> 22, of which waited for: 13 -> 16; matrix products, arithmetic and copies ran while one was open for 7% -> 8% of each run, Pallas kernels for 0% -> 0%
where the time goes in v1:
time: 801 us; the launch traced here: 800 us
  waiting for transfers between devices  495 us (62%)
  blocking collectives  175 us (22%)
  matrix products  53.8 us (7%)
  other arithmetic  35.1 us (4%)
  between operations  16.8 us (2%)
  local copies, waits for them, and re-layouts  13.5 us (2%)
  starting transfers between devices  10.7 us (1%)
    reduce_scatter x2, waiting for transfers between devices, reduce_grads(): lax.psum_scatter(first_grad, 'dp', scatter_dimension=0, tiled=True)  129 us
    reduce_scatter x2, waiting for transfers between devices, reduce_grads(): lax.psum_scatter(second_grad, 'dp', scatter_dimension=0, tiled=True)  129 us
    reduce_scatter x2, waiting for transfers between devices, reduce_grads(): lax.psum_scatter(third_grad, 'dp', scatter_dimension=0, tiled=True)  79.5 us
    psum x1, blocking collectives, on_device(): lax.psum((jnp.sum(in_terms, axis=0), jnp.sum(pa_terms, axis=0), jnp.sum(p...  45.7 us
    all_gather x1, waiting for transfers between devices, fetch_weights(): lax.all_gather(w_up, 'dp', axis=0, tiled=True)  36.1 us
    all_gather x1, waiting for transfers between devices, fetch_weights(): lax.all_gather(w_down, 'dp', axis=0, tiled=True)  34.9 us
    all_gather x1, blocking collectives, fetch_weights(): lax.all_gather(w_out, 'dp', axis=0, tiled=True)  25.3 us
    all_gather x1, blocking collectives, fetch_weights(): lax.all_gather(w_value, 'dp', axis=0, tiled=True)  23.7 us
  transfers between devices with their start and end apart: 22, of which 16 were waited for; matrix products, arithmetic and copies ran while one was open for 8% of the time, Pallas kernels for 0%

profile of v1, /device:TPU:0, one launch (start us, length us, event | category | flops | bytes accessed | tf_op | source)
XLA Modules:
  0.0 799.8 jit_solution(13552600891495246802)
XLA Ops:
  11.0 23.7 %all_gather.37 = bf16[640,256]{1,0:T(8,128)(2,1)S(1)} all-gather(bf16[40,256]{1,0:T(8,128)(2,1)} %param.29), channel_id=1, replica_groups=mesh['dp'=16,'tensor'=2] {'dp'}, dimensions={0}, use_global_device_ids=true | all-gather | bytes 348160 | tf_op jit(solution)/shard_map/all_gather | solution.py:147
  36.0 10.6 %all_gather.36 = bf16[512,640]{1,0:T(8,128)(2,1)S(1)} all-gather(bf16[256,640]{1,0:T(8,128)(2,1)S(1)} %fusion.39), channel_id=1, replica_groups=mesh['dp'=16,'tensor'=2] {'tensor'}, dimensions={0}, use_global_device_ids=true | all-gather | bytes 983040 | tf_op jit(solution)/shard_map/all_gather | solution.py:169
  49.8 18.0 %all_gather.38 = bf16[640,256]{1,0:T(8,128)(2,1)S(1)} all-gather(bf16[40,256]{1,0:T(8,128)(2,1)S(1)} %copy-done.58), channel_id=1, replica_groups=mesh['dp'=16,'tensor'=2] {'dp'}, dimensions={0}, use_global_device_ids=true | all-gather | bytes 348160 | tf_op jit(solution)/shard_map/all_gather | solution.py:146
  78.5 2.8 collective-permute-done.4
  82.9 25.3 %all_gather.39 = bf16[640,512]{1,0:T(8,128)(2,1)S(1)} all-gather(bf16[40,512]{1,0:T(8,128)(2,1)S(1)} %copy-done.55), channel_id=1, replica_groups=mesh['dp'=16,'tensor'=2] {'dp'}, dimensions={0}, use_global_device_ids=true | all-gather | bytes 696320 | tf_op jit(solution)/shard_map/all_gather | solution.py:148
  115.6 2.6 fusion.29
  122.6 23.3 %reduce-scatter.11.cloned.1.call-done = f32[256,640]{1,0:T(8,128)} async-done(((f32[512,640]{1,0:T(8,128)}), f32[256,640]{1,0:T(8,128)}) %reduce-scatter.11.cloned.1.call-update) | async-done | bytes 655376 | tf_op jit(solution)/shard_map/reduce_scatter | solution.py:206
  150.3 10.1 %all_gather.40 = bf16[512,640]{1,0:T(8,128)(2,1)S(1)} all-gather(bf16[256,640]{1,0:T(8,128)(2,1)S(1)} %multiply_convert_fusion.2), channel_id=1, replica_groups=mesh['dp'=16,'tensor'=2] {'tensor'}, dimensions={0}, use_global_device_ids=true | all-gather | bytes 983040 | tf_op jit(solution)/shard_map/all_gather | solution.py:215
  160.5 3.4 all-gather.4.cloned.1.call-done
  163.8 3.7 fusion.84
  167.5 36.1 %all-gather.6.cloned.1.call-done = bf16[640,1024]{1,0:T(8,128)(2,1)} async-done(((bf16[40,1024]{1,0:T(8,128)(2,1)}), bf16[640,1024]{1,0:T(8,128)(2,1)}) %all-gather.6.cloned.1.call-update) | async-done | bytes 1310736 | tf_op jit(solution)/shard_map/all_gather | solution.py:150
  203.6 4.9 multiply_convert_fusion.1
  208.5 34.9 %all-gather.8.cloned.1.call-done = bf16[640,1024]{1,0:T(8,128)(2,1)} async-done(((bf16[40,1024]{1,0:T(8,128)(2,1)}), bf16[640,1024]{1,0:T(8,128)(2,1)}) %all-gather.8.cloned.1.call-update) | async-done | bytes 1310736 | tf_op jit(solution)/shard_map/all_gather | solution.py:151
  243.4 3.7 fusion.85
  248.5 21.0 %reduce-scatter.13.cloned.1.call-done = f32[256,640]{1,0:T(8,128)} async-done(((f32[512,640]{1,0:T(8,128)}), f32[256,640]{1,0:T(8,128)}) %reduce-scatter.13.cloned.1.call-update) | async-done | bytes 655376 | tf_op jit(solution)/shard_map/reduce_scatter | solution.py:220
  275.0 9.9 %all_gather.44 = bf16[512,640]{1,0:T(8,128)(2,1)S(1)} all-gather(bf16[256,640]{1,0:T(8,128)(2,1)S(1)} %get-tuple-element.134), channel_id=1, replica_groups=mesh['dp'=16,'tensor'=2] {'tensor'}, dimensions={0}, use_global_device_ids=true | all-gather | bytes 983040 | tf_op jit(solution)/shard_map/all_gather | solution.py:232
  285.0 3.9 multiply_convert_fusion
  294.5 22.1 %reduce-scatter.15.cloned.1.call-done = f32[256,640]{1,0:T(8,128)} async-done(((f32[512,640]{1,0:T(8,128)}), f32[256,640]{1,0:T(8,128)}) %reduce-scatter.15.cloned.1.call-update) | async-done | bytes 655376 | tf_op jit(solution)/shard_map/reduce_scatter | solution.py:241
  321.3 10.1 %all_gather.45 = bf16[512,640]{1,0:T(8,128)(2,1)S(1)} all-gather(bf16[256,640]{1,0:T(8,128)(2,1)S(1)} %subtract_convert_fusion.1), channel_id=1, replica_groups=mesh['dp'=16,'tensor'=2] {'tensor'}, dimensions={0}, use_global_device_ids=true | all-gather | bytes 983040 | tf_op jit(solution)/shard_map/all_gather | solution.py:251
  332.2 2.7 fusion.1
  345.8 3.6 fusion.25
  350.8 7.9 collective-permute-done.7
  358.8 21.1 %all-reduce.5 = bf16[512,256]{0,1:T(8,128)(2,1)S(1)} all-reduce(f32[512,256]{0,1:T(8,128)S(1)} %slice_add_fusion), channel_id=1, replica_groups=mesh['dp'=16,'tensor'=2] {'tensor'}, use_global_device_ids=true, to_apply=%region_19.20 | all-reduce | flops 131072 | bytes 786432 | tf_op jit(solution)/shard_map/psum | solution.py:298
  384.8 3.6 fusion.92
  401.3 2.9 reduce-scatter.17.cloned.1.call-done
  406.2 45.7 %all-reduce = (f32[640]{0:T(1024)}, f32[640]{0:T(1024)}, f32[640]{0:T(1024)}, f32[640]{0:T(1024)}, f32[256]{0:T(256)}, /*index=5*/f32[256]{0:T(256)}) all-reduce(f32[640]{0:T(1024)S(1)} %get-tuple-element.117, f32[640]{0:T(1024)S(1)} %copy-done.69, f32[640]{0:T(1024)S(1)} %copy-done.68, ...), channel_id=1, replica_groups=mesh['dp'=16,'tensor'=2] {'dp','tensor'}, use_global_device_ids=true, to_apply=%region_28.29 | all-reduce | flops 3072 | bytes 24576 | tf_op jit(solution)/shard_map/psum | solution.py:327
  452.9 13.3 %reduce-scatter.21.cloned.1.call-done = f32[40,512]{1,0:T(8,128)} async-done(((f32[640,512]{1,0:T(8,128)}), f32[40,512]{1,0:T(8,128)}) %reduce-scatter.21.cloned.1.call-update) | async-done | bytes 81936 | tf_op jit(solution)/shard_map/reduce_scatter | solution.py:158
  467.7 66.2 %reduce-scatter.29.cloned.1.call-done = f32[40,1024]{1,0:T(8,128)} async-done(((f32[640,1024]{1,0:T(8,128)}), f32[40,1024]{1,0:T(8,128)}) %reduce-scatter.29.cloned.1.call-update) | async-done | bytes 163856 | tf_op jit(solution)/shard_map/reduce_scatter | solution.py:158
  533.9 67.6 %reduce-scatter.27.cloned.1.call-done = f32[40,1024]{1,0:T(8,128)} async-done(((f32[640,1024]{1,0:T(8,128)}), f32[40,1024]{1,0:T(8,128)}) %reduce-scatter.27.cloned.1.call-update) | async-done | bytes 163856 | tf_op jit(solution)/shard_map/reduce_scatter | solution.py:157
  601.4 67.6 %reduce-scatter.25.cloned.1.call-done = f32[40,1024]{1,0:T(8,128)} async-done(((f32[640,1024]{1,0:T(8,128)}), f32[40,1024]{1,0:T(8,128)}) %reduce-scatter.25.cloned.1.call-update) | async-done | bytes 163856 | tf_op jit(solution)/shard_map/reduce_scatter | solution.py:156
  669.0 61.6 %reduce-scatter.23.cloned.1.call-done = f32[40,512]{1,0:T(8,128)} async-done(((f32[640,512]{1,0:T(8,128)}), f32[40,512]{1,0:T(8,128)}) %reduce-scatter.23.cloned.1.call-update) | async-done | bytes 81936 | tf_op jit(solution)/shard_map/reduce_scatter | solution.py:157
  730.6 61.9 %reduce-scatter.19.cloned.1.call-done = f32[40,512]{1,0:T(8,128)} async-done(((f32[640,512]{1,0:T(8,128)}), f32[40,512]{1,0:T(8,128)}) %reduce-scatter.19.cloned.1.call-update) | async-done | bytes 81936 | tf_op jit(solution)/shard_map/reduce_scatter | solution.py:156
  (313 shorter events, 87.5 us)
Async XLA Ops:
  8.0 41.8 %copy-start.89 = (bf16[256]{0:T(256)(128)(2,1)S(1)}, bf16[256]{0:T(256)(128)(2,1)}, u32[]{:S(2)}) copy-start(bf16[256]{0:T(256)(128)(2,1)} %param.39) | copy-start | bytes 1540
  8.0 41.8 %copy-start.58 = (bf16[40,256]{1,0:T(8,128)(2,1)S(1)}, bf16[40,256]{1,0:T(8,128)(2,1)}, u32[]{:S(2)}) copy-start(bf16[40,256]{1,0:T(8,128)(2,1)} %param.28) | copy-start | bytes 61444
  8.0 137.8 %reduce-scatter.11.cloned.1.call-start = ((), (), s32[]{:S(2)}) async-start(), calls=%async_computation.10 | async-start | bytes 1966080 | tf_op jit(solution)/shard_map/reduce_scatter | solution.py:206
  8.1 61.7 %collective-permute-start.2 = (bf16[1,40,512]{2,1,0:T(8,128)(2,1)}, bf16[1,40,512]{2,1,0:T(8,128)(2,1)S(1)}, u32[]{:S(2)}, u32[]{:S(2)}) collective-permute-start(bf16[1,40,512]{2,1,0:T(8,128)(2,1)} %bitcast.113), channel_id=1, source_target_pairs={{0,2},{2,0},{4,6},{6,4},{8,10},{10,8},{12,14},{14,12},{16,18},{18,... | collective-permute-start | bytes 122888 | tf_op jit(solution)/shard_map/ppermute | solution.py:23
  10.3 39.5 %copy-start.61 = (f32[256]{0:T(256)}, f32[256]{0:T(256)S(1)}, u32[]{:S(2)}) copy-start(f32[256]{0:T(256)S(1)} %get-tuple-element.157) | copy-start | bytes 3076
  47.7 66.9 %collective-permute-start = (bf16[512,256]{1,0:T(8,128)(2,1)}, bf16[512,256]{1,0:T(8,128)(2,1)}, u32[]{:S(2)}, u32[]{:S(2)}) collective-permute-start(bf16[512,256]{1,0:T(8,128)(2,1)} %convolution_convert_fusion.1), channel_id=1, source_target_pairs={{0,2},{2,4},{4,6},{6,8},{8,10},{10,12},{12,14},{14,16},{16,18},{18... | collective-permute-start | bytes 786440 | tf_op jit(solution)/shard_map/ppermute | solution.py:37
  70.2 5.0 collective-permute-start.3
  74.2 34.0 %copy-start.47 = (bf16[512,128]{0,1:T(8,128)(2,1)}, bf16[512,128]{0,1:T(8,128)(2,1)S(1)}, u32[]{:S(2)}) copy-start(bf16[512,128]{0,1:T(8,128)(2,1)S(1)} %get-tuple-element.141) | copy-start | bytes 393220
  74.2 34.1 %copy-start.44 = (bf16[512,128]{0,1:T(8,128)(2,1)}, bf16[512,128]{0,1:T(8,128)(2,1)S(1)}, u32[]{:S(2)}) copy-start(bf16[512,128]{0,1:T(8,128)(2,1)S(1)} %get-tuple-element.140) | copy-start | bytes 393220
  75.3 5.9 collective-permute-start.4
  76.1 34.9 %collective-permute-start.1 = (bf16[512,256]{0,1:T(8,128)(2,1)}, bf16[512,256]{0,1:T(8,128)(2,1)}, u32[]{:S(2)}, u32[]{:S(2)}) collective-permute-start(bf16[512,256]{0,1:T(8,128)(2,1)} %pad_maximum_fusion.9), channel_id=1, source_target_pairs={{0,2},{2,4},{4,6},{6,8},{8,10},{10,12},{12,14},{14,16},{16,18},{18... | collective-permute-start | bytes 786440 | tf_op jit(solution)/shard_map/ppermute | solution.py:37
  81.3 26.9 %collective-permute-start.5 = (bf16[8,40,512]{2,1,0:T(8,128)(2,1)S(1)}, bf16[8,40,512]{2,1,0:T(8,128)(2,1)S(1)}, u32[]{:S(2)}, u32[]{:S(2)}) collective-permute-start(bf16[8,40,512]{2,1,0:T(8,128)(2,1)S(1)} %pad_maximum_fusion.8), channel_id=1, source_target_pairs={{0,16},{2,18},{4,20},{6,22},{8,24},{10,26},{12,28},{14,30},{16,0},... | collective-permute-start | bytes 983048 | tf_op jit(solution)/shard_map/ppermute | solution.py:23
  120.7 43.1 %all-gather.4.cloned.1.call-start = ((), (), s32[]{:S(2)}) async-start(), calls=%async_computation.11 | async-start | bytes 1392640 | tf_op jit(solution)/shard_map/all_gather | solution.py:149
  121.3 82.3 %all-gather.6.cloned.1.call-start = ((), (), s32[]{:S(2)}) async-start(), calls=%async_computation.12 | async-start | bytes 1392640 | tf_op jit(solution)/shard_map/all_gather | solution.py:150
  121.9 121.5 %all-gather.8.cloned.1.call-start = ((), (), s32[]{:S(2)}) async-start(), calls=%async_computation.13 | async-start | bytes 1392640 | tf_op jit(solution)/shard_map/all_gather | solution.py:151
  122.5 147.0 %reduce-scatter.13.cloned.1.call-start = ((), (), s32[]{:S(2)}) async-start(), calls=%async_computation.14 | async-start | bytes 1966080 | tf_op jit(solution)/shard_map/reduce_scatter | solution.py:220
  247.2 69.4 %reduce-scatter.15.cloned.1.call-start = ((), (), s32[]{:S(2)}) async-start(), calls=%async_computation.15 | async-start | bytes 1966080 | tf_op jit(solution)/shard_map/reduce_scatter | solution.py:241
  293.1 86.8 %all-reduce.4.cloned.1.call-start = ((), (), s32[]{:S(2)}) async-start(), calls=%async_computation.17 | async-start | bytes 1048576 | tf_op jit(solution)/shard_map/psum | solution.py:298
  335.8 4.7 collective-permute-start.6
  341.4 62.7 %reduce-scatter.17.cloned.1.call-start = ((), (), s32[]{:S(2)}) async-start(), calls=%async_computation.16 | async-start | bytes 1966080 | tf_op jit(solution)/shard_map/reduce_scatter | solution.py:310
  345.5 120.7 %reduce-scatter.21.cloned.1.call-start = ((), (), s32[]{:S(2)}) async-start(), calls=%async_computation.19 | async-start | bytes 1392640 | tf_op jit(solution)/shard_map/reduce_scatter | solution.py:158
  349.4 32.7 %copy-start.75 = (f32[256]{0:T(256)S(1)}, f32[256]{0:T(256)}, u32[]{:S(2)}) copy-start(f32[256]{0:T(256)} %copy-done.74) | copy-start | bytes 3076
  349.5 32.8 %copy-start.57 = (f32[512]{0:T(512)S(1)}, f32[512]{0:T(512)}, u32[]{:S(2)}) copy-start(f32[512]{0:T(512)} %copy-done.56) | copy-start | bytes 6148
  349.5 32.8 %copy-start.76 = (f32[512]{0:T(512)S(1)}, f32[512]{0:T(512)}, u32[]{:S(2)}) copy-start(f32[512]{0:T(512)} %get-tuple-element.154) | copy-start | bytes 6148
  349.5 9.2 %collective-permute-start.7 = (f32[512,256]{0,1:T(8,128)S(1)}, f32[512,256]{0,1:T(8,128)S(1)}, u32[]{:S(2)}, u32[]{:S(2)}) collective-permute-start(f32[512,256]{0,1:T(8,128)S(1)} %slice.103), channel_id=1, source_target_pairs={{2,0},{4,2},{6,4},{8,6},{10,8},{12,10},{14,12},{16,14},{18,16},{20... | collective-permute-start | bytes 1572872 | tf_op jit(solution)/shard_map/ppermute | solution.py:37
  384.8 149.1 %reduce-scatter.29.cloned.1.call-start = ((), (), s32[]{:S(2)}) async-start(), calls=%async_computation.23 | async-start | bytes 2785280 | tf_op jit(solution)/shard_map/reduce_scatter | solution.py:158
  388.4 213.0 %reduce-scatter.27.cloned.1.call-start = ((), (), s32[]{:S(2)}) async-start(), calls=%async_computation.22 | async-start | bytes 2785280 | tf_op jit(solution)/shard_map/reduce_scatter | solution.py:157
  392.0 277.0 %reduce-scatter.25.cloned.1.call-start = ((), (), s32[]{:S(2)}) async-start(), calls=%async_computation.21 | async-start | bytes 2785280 | tf_op jit(solution)/shard_map/reduce_scatter | solution.py:156
  395.7 334.9 %reduce-scatter.23.cloned.1.call-start = ((), (), s32[]{:S(2)}) async-start(), calls=%async_computation.20 | async-start | bytes 1392640 | tf_op jit(solution)/shard_map/reduce_scatter | solution.py:157
  398.6 393.9 %reduce-scatter.19.cloned.1.call-start = ((), (), s32[]{:S(2)}) async-start(), calls=%async_computation.18 | async-start | bytes 1392640 | tf_op jit(solution)/shard_map/reduce_scatter | solution.py:156
  401.3 50.6 %copy-start.4 = (f32[256,640]{1,0:T(8,128)S(1)}, f32[256,640]{1,0:T(8,128)}, u32[]{:S(2)}) copy-start(f32[256,640]{1,0:T(8,128)} %copy-done.3) | copy-start | bytes 1966084
  401.3 50.6 %copy-start.78 = (f32[256]{0:T(256)S(1)}, f32[256]{0:T(256)}, u32[]{:S(2)}) copy-start(f32[256]{0:T(256)} %get-tuple-element.156) | copy-start | bytes 3076
  (84 other events, 520.2 us)
Sparse Core Ops, SparseCore 0:
  120.8 24.9 reduce-scatter.10
  247.3 22.1 reduce-scatter.12
  293.2 23.2 reduce-scatter.14
  341.5 38.2 all-reduce.3
  382.0 22.1 reduce-scatter.16
  407.6 58.5 reduce-scatter.20
  470.6 63.2 reduce-scatter.28
  538.2 63.1 reduce-scatter.26
  605.8 63.1 reduce-scatter.24
  673.1 57.5 reduce-scatter.22
  734.8 57.6 reduce-scatter.18
Sparse Core Ops, SparseCore 1:
  123.5 40.3 all-gather.3
  166.0 37.6 all-gather.5
  205.8 37.6 all-gather.7
